TPU v7x, 256 devices: a whole 4x4x8 slice. The times are simulated.
256 devices in a mesh: leaf: 32 (over z, x), rank: 4 (over y), rhs: 2 (over core).
Axes of the slice: x: 4, y: 4, z: 8, core: 2. Of those that a mesh axis runs over, the one named last changes fastest.
Arguments:
- rhs: float32 [65536, 512], P(('leaf', 'rank'), 'rhs'), parts along dimension 1, may hold values from -40 to 40
- order: int32 [65536], P(('leaf', 'rank')), may hold values from 0 to 65535, as said below
- diag: float32 [65536], P(('leaf', 'rank')), may hold values from 2 to 8
- blocks: bfloat16 [1536, 128, 128], P(('leaf', 'rank')), may hold values from -0.3125 to 0.3125
- near_rows: int32 [1536], P(('leaf', 'rank')), may hold values from 0 to 511, as said below
- near_cols: int32 [1536], P(('leaf', 'rank')), may hold values from 0 to 511, as said below
- gen_u: bfloat16 [5, 65536, 128], P(None, 'leaf', 'rank'), may hold values from -0.5 to 0.5
- gen_v: bfloat16 [5, 65536, 128], P(None, 'leaf', 'rank'), may hold values from -0.03125 to 0.03125
Outputs:
- solution: float32 [65536, 512], P(('leaf', 'rank'), 'rhs'), parts along dimension 1
- residual: float32 [65536, 512], P(('leaf', 'rank'), 'rhs'), parts along dimension 1
There are 2 independent parts, one for each index of `rhs`. A program takes and returns all parts, laid end to end along the dimension named above; an argument that names none is the same for every part. Nothing has to cross between parts.
Inputs may be any that keep to these rules, and one draw needn't show every extreme that they name: `order`: each aligned run of 512 entries is a permutation of the panel numbers of that run. `near_rows`: block k's row is one of the 4 block rows of the device that holds block k; every block row is named, at least once by a block whose column equals it. `near_cols`: block k's column lies in the same subtree of 2048 panels as its row, at most 4 block columns away from it.
All inputs are finite; a program needn't handle non-finite values.
Results may differ from a plain program's by a relative error of at most 0.0035.
Values may be sent and summed in bfloat16 or wider, within the bound.
A program may use at most 64 MiB of HBM per device.

v0:
```python
import jax
import jax.numpy as jnp
from jax import lax
from jax.sharding import PartitionSpec as P

EPSILON = 1e-06


def from_partner(value, axis, apart):
    mask = 2**apart
    pairs = [(source, source ^ mask) for source in range(lax.axis_size(axis))]
    return lax.ppermute(value, axis, pairs)


def local(rhs, order, diag, blocks, near_rows, near_cols, gen_u, gen_v):
    panel_count, columns_count = rhs.shape
    levels = gen_v.shape[0]
    leaf_panels = gen_v.shape[1]
    block_size = blocks.shape[1]
    rows_dev = panel_count // block_size
    rows_leaf = leaf_panels // block_size
    device = lax.axis_index(("leaf", "rank"))
    leaf_id = lax.axis_index("leaf")
    local_order = order - device * panel_count
    local_rows = near_rows - device * rows_dev
    local_cols = near_cols - leaf_id * rows_leaf
    selector = (jnp.arange(rows_dev, dtype=jnp.int32)[:, None] == local_rows[None, :]).astype(
        jnp.float32
    )

    def tree_sums(coeffs):
        partial_value = [coeffs[level] for level in range(levels)]
        sibling = []
        for level in range(levels):
            stacked = jnp.stack(partial_value[level:], 0)
            received = from_partner(stacked, "leaf", level)
            sibling.append(received[0])
            for upper in range(level + 1, levels):
                partial_value[upper] = partial_value[upper] + received[upper - level]
        return jnp.stack(sibling, 0)

    def apply(vector):
        narrow = vector.astype(jnp.bfloat16)
        subtree = lax.all_gather(narrow, "rank", axis=0, tiled=True)
        coeffs = jnp.einsum("lpk,pn->lkn", gen_v, subtree, preferred_element_type=jnp.float32)
        column_blocks = subtree.reshape(rows_leaf, block_size, columns_count)[local_cols]
        sibling = tree_sums(coeffs).astype(jnp.bfloat16)
        products = jnp.einsum(
            "kij,kjn->kin", blocks, column_blocks, preferred_element_type=jnp.float32
        )
        near = jnp.einsum(
            "rk,kin->rin", selector, products, precision=lax.Precision.HIGHEST
        ).reshape(panel_count, columns_count)
        far = lax.psum_scatter(
            jnp.einsum("lpk,lkn->pn", gen_u, sibling, preferred_element_type=jnp.float32),
            "rank",
            scatter_dimension=0,
            tiled=True,
        )
        return diag[:, None] * vector + near + far

    start = rhs[local_order]
    beta = jnp.sqrt(lax.psum(jnp.sum(start * start, axis=0), ("leaf", "rank")) + EPSILON)
    basis_one = start / beta
    image_one = apply(basis_one)
    h11 = lax.psum(jnp.sum(basis_one * image_one, axis=0), ("leaf", "rank"))
    rest_one = image_one - h11 * basis_one
    h21 = jnp.sqrt(lax.psum(jnp.sum(rest_one * rest_one, axis=0), ("leaf", "rank")) + EPSILON)
    basis_two = rest_one / h21
    image_two = apply(basis_two)
    h12, h22 = lax.psum(
        (jnp.sum(basis_one * image_two, axis=0), jnp.sum(basis_two * image_two, axis=0)),
        ("leaf", "rank"),
    )
    rest_two = image_two - h12 * basis_one - h22 * basis_two
    h32 = jnp.sqrt(lax.psum(jnp.sum(rest_two * rest_two, axis=0), ("leaf", "rank")) + EPSILON)
    r_one = jnp.sqrt(h11 * h11 + h21 * h21)
    cos_one = h11 / r_one
    sin_one = h21 / r_one
    top = cos_one * h12 + sin_one * h22
    low = cos_one * h22 - sin_one * h12
    r_two = jnp.sqrt(low * low + h32 * h32)
    y_two = low / r_two * (-sin_one * beta) / r_two
    y_one = (cos_one * beta - top * y_two) / r_one
    tree_solution = y_one * basis_one + y_two * basis_two
    tree_residual = (
        (beta - y_one * h11 - y_two * h12) * basis_one
        - (y_one * h21 + y_two * h22) * basis_two
        - y_two * rest_two
    )
    solution = jnp.zeros_like(rhs).at[local_order].set(tree_solution)
    residual = jnp.zeros_like(rhs).at[local_order].set(tree_residual)
    return (solution, residual)


def solution(mesh):
    in_specs = (
        P(("leaf", "rank"), "rhs"),
        P(("leaf", "rank")),
        P(("leaf", "rank")),
        P(("leaf", "rank"), None, None),
        P(("leaf", "rank")),
        P(("leaf", "rank")),
        P(None, "leaf", "rank"),
        P(None, "leaf", "rank"),
    )
    out_specs = (P(("leaf", "rank"), "rhs"), P(("leaf", "rank"), "rhs"))
    return jax.shard_map(local, mesh=mesh, in_specs=in_specs, out_specs=out_specs, check_vma=False)
```

profile of v0, /device:TPU:8, one launch (start us, length us, event | category | flops | bytes accessed | tf_op | source)
XLA Modules:
  0.0 1938.2 jit_solution(10514694611025003767)
XLA Ops:
  8.0 2.7 gather_fusion
  10.8 346.4 %psum.42 = f32[256]{0:T(256)S(1)} all-reduce(f32[256]{0:T(256)S(1)} %multiply_reduce_fusion.5), channel_id=1, replica_groups=mesh['leaf'=32,'rank'=4,'rhs'=2] {'leaf','rank'}, use_global_device_ids=true, to_apply=%region_1.0 | all-reduce | flops 256 | bytes 2048 | tf_op jit(solution)/shard_map/psum | solution.py:63
  357.9 23.9 %all-gather.3.cloned.1.call-done = bf16[2048,256]{1,0:T(8,128)(2,1)} async-done(((bf16[512,256]{1,0:T(8,128)(2,1)}), bf16[2048,256]{1,0:T(8,128)(2,1)}) %all-gather.3.cloned.1.call-update) | async-done | bytes 1048592 | tf_op jit(solution)/shard_map/all_gather | solution.py:44
  385.0 3.9 collective-permute-done
  388.9 3.1 collective-permute-start.1
  391.9 3.5 collective-permute-done.1
  397.1 3.8 collective-permute-done.2
  402.8 3.3 collective-permute-done.3
  406.2 6.2 collective-permute-start.4
  421.8 27.5 %reduce-scatter.3.cloned.1.call-done = f32[512,256]{1,0:T(8,128)} async-done(((f32[2048,256]{1,0:T(8,128)}), f32[512,256]{1,0:T(8,128)}) %reduce-scatter.3.cloned.1.call-update) | async-done | bytes 524304 | tf_op jit(solution)/shard_map/reduce_scatter | solution.py:54
  450.5 344.0 %psum.43 = f32[256]{0:T(256)S(1)} all-reduce(f32[256]{0:T(256)S(1)} %multiply_reduce_fusion.4), channel_id=1, replica_groups=mesh['leaf'=32,'rank'=4,'rhs'=2] {'leaf','rank'}, use_global_device_ids=true, to_apply=%region_4.0 | all-reduce | flops 256 | bytes 2048 | tf_op jit(solution)/shard_map/psum | solution.py:66
  795.7 347.8 %psum.44 = f32[256]{0:T(256)S(1)} all-reduce(f32[256]{0:T(256)S(1)} %get-tuple-element.10), channel_id=1, replica_groups=mesh['leaf'=32,'rank'=4,'rhs'=2] {'leaf','rank'}, use_global_device_ids=true, to_apply=%region_6.0 | all-reduce | flops 256 | bytes 2048 | tf_op jit(solution)/shard_map/psum | solution.py:68
  1144.4 20.1 %all-gather.5.cloned.1.call-done = bf16[2048,256]{1,0:T(8,128)(2,1)} async-done(((bf16[512,256]{1,0:T(8,128)(2,1)}), bf16[2048,256]{1,0:T(8,128)(2,1)}) %all-gather.5.cloned.1.call-update) | async-done | bytes 1048592 | tf_op jit(solution)/shard_map/all_gather | solution.py:44
  1167.6 3.9 collective-permute-done.5
  1171.5 3.1 collective-permute-start.6
  1174.6 3.5 collective-permute-done.6
  1179.7 3.8 collective-permute-done.7
  1185.4 3.3 collective-permute-done.8
  1188.8 6.4 collective-permute-start.9
  1206.5 25.5 %reduce-scatter.5.cloned.1.call-done = f32[512,256]{1,0:T(8,128)} async-done(((f32[2048,256]{1,0:T(8,128)}), f32[512,256]{1,0:T(8,128)}) %reduce-scatter.5.cloned.1.call-update) | async-done | bytes 524304 | tf_op jit(solution)/shard_map/reduce_scatter | solution.py:54
  1233.3 344.0 %all-reduce = (f32[256]{0:T(256)S(1)}, f32[256]{0:T(256)S(1)}) all-reduce(f32[256]{0:T(256)S(1)} %get-tuple-element.3, f32[256]{0:T(256)S(1)} %get-tuple-element.2), channel_id=1, replica_groups=mesh['leaf'=32,'rank'=4,'rhs'=2] {'leaf','rank'}, use_global_device_ids=true, to_apply=%region_11.0 | all-reduce | flops 512 | bytes 4096 | tf_op jit(solution)/shard_map/psum | solution.py:71
  1577.5 347.8 %psum.47 = f32[256]{0:T(256)S(1)} all-reduce(f32[256]{0:T(256)S(1)} %multiply_reduce_fusion), channel_id=1, replica_groups=mesh['leaf'=32,'rank'=4,'rhs'=2] {'leaf','rank'}, use_global_device_ids=true, to_apply=%region_13.0 | all-reduce | flops 256 | bytes 2048 | tf_op jit(solution)/shard_map/psum | solution.py:76
  1925.3 3.1 scatter_custom_fusion
  1928.4 3.2 scatter_custom_fusion.1
  (86 shorter events, 40.5 us)
Async XLA Ops:
  7.2 407.0 %copy-start = (bf16[5,2048,32]{1,2,0:T(8,128)(2,1)S(1)}, bf16[5,2048,32]{1,2,0:T(8,128)(2,1)}, u32[]{:S(2)}) copy-start(bf16[5,2048,32]{1,2,0:T(8,128)(2,1)} %param.14) | copy-start | bytes 1966084
  7.2 374.7 %all-gather.3.cloned.1.call-start = ((), (), s32[]{:S(2)}) async-start(), calls=%async_computation.2 | async-start | bytes 1310720 | tf_op jit(solution)/shard_map/all_gather | solution.py:44
  8.0 373.9 %copy-start.3 = (bf16[5,2048,32]{1,2,0:T(8,128)(2,1)S(1)}, bf16[5,2048,32]{1,2,0:T(8,128)(2,1)}, u32[]{:S(2)}) copy-start(bf16[5,2048,32]{1,2,0:T(8,128)(2,1)} %param.15) | copy-start | bytes 1966084
  357.9 91.4 %reduce-scatter.3.cloned.1.call-start = ((), (), s32[]{:S(2)}) async-start(), calls=%async_computation.3 | async-start | bytes 2621440 | tf_op jit(solution)/shard_map/reduce_scatter | solution.py:54
  383.4 5.4 collective-permute-start
  388.9 6.6 collective-permute-start.1
  395.5 5.4 collective-permute-start.2
  400.9 5.3 collective-permute-start.3
  406.2 8.0 collective-permute-start.4
  414.1 2.0 copy-start.7
  414.1 2.0 copy-start.8
  414.2 2.0 copy-start.1
  416.1 1.0 copy-start.5
  416.1 748.4 %all-gather.5.cloned.1.call-start = ((), (), s32[]{:S(2)}) async-start(), calls=%async_computation.4 | async-start | bytes 1310720 | tf_op jit(solution)/shard_map/all_gather | solution.py:44
  420.8 28.5 %copy-start.6 = (f32[512]{0:T(512)S(1)}, f32[512]{0:T(512)}, u32[]{:S(2)}) copy-start(f32[512]{0:T(512)} %param.10) | copy-start | bytes 6148
  421.8 742.7 %copy-start.4 = (bf16[5,2048,32]{1,2,0:T(8,128)(2,1)S(1)}, bf16[5,2048,32]{1,2,0:T(8,128)(2,1)}, u32[]{:S(2)}) copy-start(bf16[5,2048,32]{1,2,0:T(8,128)(2,1)} %param.15) | copy-start | bytes 1966084
  1144.3 87.8 %reduce-scatter.5.cloned.1.call-start = ((), (), s32[]{:S(2)}) async-start(), calls=%async_computation.5 | async-start | bytes 2621440 | tf_op jit(solution)/shard_map/reduce_scatter | solution.py:54
  1166.0 5.4 collective-permute-start.5
  1171.5 6.6 collective-permute-start.6
  1178.1 5.4 collective-permute-start.7
  1183.5 5.3 collective-permute-start.8
  1188.8 8.1 collective-permute-start.9
  1196.9 1.9 copy-start.2
Sparse Core Ops, SparseCore 0:
  358.0 23.7 all-gather.2
  416.2 33.0 reduce-scatter.2
  1144.4 20.0 all-gather.4
  1199.0 33.0 reduce-scatter.4
where the time goes:
time: 1940 us
  blocking collectives  1730 us (89%)
  waiting for transfers between devices  129 us (7%)
  starting transfers between devices  29.2 us (2%)
    psum x1, blocking collectives, local(): lax.psum(jnp.sum(rest_one * rest_one, axis=0), ('leaf', 'rank')) + EPSILON  348 us
    psum x1, blocking collectives, local(): lax.psum(jnp.sum(rest_two * rest_two, axis=0), ('leaf', 'rank')) + EPSILON  348 us
    psum x1, blocking collectives, local(): lax.psum(jnp.sum(start * start, axis=0), ('leaf', 'rank')) + EPSILON  346 us
    psum x1, blocking collectives, local(): lax.psum((jnp.sum(basis_one * image_two, axis=0), jnp.sum(basis_two * ima...  344 us
    psum x1, blocking collectives, local(): h11 = lax.psum(jnp.sum(basis_one * image_one, axis=0), ('leaf', 'rank'))  344 us
    reduce_scatter x2, waiting for transfers between devices, apply(): lax.psum_scatter(jnp.einsum('lpk,lkn->pn', gen_u, sibling, preferred_elem...  53 us
    all_gather x2, waiting for transfers between devices, apply(): subtree = lax.all_gather(narrow, 'rank', axis=0, tiled=True)  44 us
  transfers between devices with their start and end apart: 14, of which 14 were waited for; matrix products, arithmetic and copies ran while one was open for 1% of the time, Pallas kernels for 0%

commit v1 on v0

--- a/solution.py
+++ b/solution.py
@@ -68,9 +68,12 @@
     h21 = jnp.sqrt(lax.psum(jnp.sum(rest_one * rest_one, axis=0), ("leaf", "rank")) + EPSILON)
     basis_two = rest_one / h21
     image_two = apply(basis_two)
-    h12, h22 = lax.psum(
-        (jnp.sum(basis_one * image_two, axis=0), jnp.sum(basis_two * image_two, axis=0)),
-        ("leaf", "rank"),
+
+    def serve_layers_all(base_x):
+        return jax.lax.psum(jax.lax.psum(base_x, axis_name="rank"), "leaf")
+
+    h12, h22 = serve_layers_all(
+        (jnp.sum(basis_one * image_two, axis=0), jnp.sum(basis_two * image_two, axis=0))
     )
     rest_two = image_two - h12 * basis_one - h22 * basis_two
     h32 = jnp.sqrt(lax.psum(jnp.sum(rest_two * rest_two, axis=0), ("leaf", "rank")) + EPSILON)

time: 1940 us -> 1670 us (0.86)
  blocking collectives: 1730 us -> 1470 us
    psum x1 -> x2, blocking collectives: 344 us -> 84.6 us  [serve_layers_all(): return jax.lax.psum(jax.lax.psum(base_x, axis_name='rank'), 'leaf')]
where the time goes in v1:
time: 1670 us
  blocking collectives  1470 us (88%)
  waiting for transfers between devices  129 us (8%)
  starting transfers between devices  29.2 us (2%)
    psum x1, blocking collectives, local(): lax.psum(jnp.sum(rest_one * rest_one, axis=0), ('leaf', 'rank')) + EPSILON  348 us
    psum x1, blocking collectives, local(): lax.psum(jnp.sum(start * start, axis=0), ('leaf', 'rank')) + EPSILON  346 us
    psum x1, blocking collectives, local(): h11 = lax.psum(jnp.sum(basis_one * image_one, axis=0), ('leaf', 'rank'))  344 us
    psum x1, blocking collectives, local(): lax.psum(jnp.sum(rest_two * rest_two, axis=0), ('leaf', 'rank')) + EPSILON  343 us
    psum x2, blocking collectives, serve_layers_all(): return jax.lax.psum(jax.lax.psum(base_x, axis_name='rank'), 'leaf')  84.6 us
    reduce_scatter x2, waiting for transfers between devices, apply(): lax.psum_scatter(jnp.einsum('lpk,lkn->pn', gen_u, sibling, preferred_elem...  53 us
    all_gather x2, waiting for transfers between devices, apply(): subtree = lax.all_gather(narrow, 'rank', axis=0, tiled=True)  44 us
  transfers between devices with their start and end apart: 14, of which 14 were waited for; matrix products, arithmetic and copies ran while one was open for 1% of the time, Pallas kernels for 0%

profile of v1, /device:TPU:8, one launch (start us, length us, event | category | flops | bytes accessed | tf_op | source)
XLA Modules:
  0.0 1674.0 jit_solution(6604439461903654605)
XLA Ops:
  10.8 346.4 %psum.56 = f32[256]{0:T(256)S(1)} all-reduce(f32[256]{0:T(256)S(1)} %multiply_reduce_fusion.5), channel_id=1, replica_groups=mesh['leaf'=32,'rank'=4,'rhs'=2] {'leaf','rank'}, use_global_device_ids=true, to_apply=%region_1.0 | all-reduce | flops 256 | bytes 2048 | tf_op jit(solution)/shard_map/psum | solution.py:63
  357.9 23.9 %all-gather.3.cloned.1.call-done = bf16[2048,256]{1,0:T(8,128)(2,1)} async-done(((bf16[512,256]{1,0:T(8,128)(2,1)}), bf16[2048,256]{1,0:T(8,128)(2,1)}) %all-gather.3.cloned.1.call-update) | async-done | bytes 1048592 | tf_op jit(solution)/shard_map/all_gather | solution.py:44
  385.0 3.9 collective-permute-done
  388.9 3.1 collective-permute-start.1
  391.9 3.5 collective-permute-done.1
  397.1 3.8 collective-permute-done.2
  402.8 3.3 collective-permute-done.3
  406.2 6.2 collective-permute-start.4
  421.8 27.5 %reduce-scatter.3.cloned.1.call-done = f32[512,256]{1,0:T(8,128)} async-done(((f32[2048,256]{1,0:T(8,128)}), f32[512,256]{1,0:T(8,128)}) %reduce-scatter.3.cloned.1.call-update) | async-done | bytes 524304 | tf_op jit(solution)/shard_map/reduce_scatter | solution.py:54
  450.5 344.0 %psum.57 = f32[256]{0:T(256)S(1)} all-reduce(f32[256]{0:T(256)S(1)} %multiply_reduce_fusion.4), channel_id=1, replica_groups=mesh['leaf'=32,'rank'=4,'rhs'=2] {'leaf','rank'}, use_global_device_ids=true, to_apply=%region_4.0 | all-reduce | flops 256 | bytes 2048 | tf_op jit(solution)/shard_map/psum | solution.py:66
  795.7 347.8 %psum.58 = f32[256]{0:T(256)S(1)} all-reduce(f32[256]{0:T(256)S(1)} %get-tuple-element.12), channel_id=1, replica_groups=mesh['leaf'=32,'rank'=4,'rhs'=2] {'leaf','rank'}, use_global_device_ids=true, to_apply=%region_6.0 | all-reduce | flops 256 | bytes 2048 | tf_op jit(solution)/shard_map/psum | solution.py:68
  1144.4 20.1 %all-gather.5.cloned.1.call-done = bf16[2048,256]{1,0:T(8,128)(2,1)} async-done(((bf16[512,256]{1,0:T(8,128)(2,1)}), bf16[2048,256]{1,0:T(8,128)(2,1)}) %all-gather.5.cloned.1.call-update) | async-done | bytes 1048592 | tf_op jit(solution)/shard_map/all_gather | solution.py:44
  1167.6 3.8 collective-permute-done.5
  1171.5 3.1 collective-permute-start.6
  1174.6 3.5 collective-permute-done.6
  1179.7 3.8 collective-permute-done.7
  1185.5 3.3 collective-permute-done.8
  1188.8 6.4 collective-permute-start.9
  1206.5 25.6 %reduce-scatter.5.cloned.1.call-done = f32[512,256]{1,0:T(8,128)} async-done(((f32[2048,256]{1,0:T(8,128)}), f32[512,256]{1,0:T(8,128)}) %reduce-scatter.5.cloned.1.call-update) | async-done | bytes 524304 | tf_op jit(solution)/shard_map/reduce_scatter | solution.py:54
  1233.3 9.5 all-reduce.1
  1242.9 75.0 %all-reduce = (f32[256]{0:T(256)S(1)}, f32[256]{0:T(256)S(1)}) all-reduce(f32[256]{0:T(256)S(1)} %get-tuple-element.6, f32[256]{0:T(256)S(1)} %get-tuple-element.7), channel_id=1, replica_groups=mesh['leaf'=32,'rank'=4,'rhs'=2] {'leaf'}, use_global_device_ids=true, to_apply=%region_13.0 | all-reduce | flops 512 | bytes 4096 | tf_op jit(solution)/shard_map/psum | solution.py:73
  1318.1 343.0 %psum.63 = f32[256]{0:T(256)S(1)} all-reduce(f32[256]{0:T(256)S(1)} %multiply_reduce_fusion), channel_id=1, replica_groups=mesh['leaf'=32,'rank'=4,'rhs'=2] {'leaf','rank'}, use_global_device_ids=true, to_apply=%region_15.0 | all-reduce | flops 256 | bytes 2048 | tf_op jit(solution)/shard_map/psum | solution.py:79
  1661.1 3.1 scatter_custom_fusion
  1664.2 3.2 scatter_custom_fusion.1
  (87 shorter events, 43.2 us)
Async XLA Ops:
  7.2 407.0 %copy-start = (bf16[5,2048,32]{1,2,0:T(8,128)(2,1)S(1)}, bf16[5,2048,32]{1,2,0:T(8,128)(2,1)}, u32[]{:S(2)}) copy-start(bf16[5,2048,32]{1,2,0:T(8,128)(2,1)} %param.14) | copy-start | bytes 1966084
  7.2 374.7 %all-gather.3.cloned.1.call-start = ((), (), s32[]{:S(2)}) async-start(), calls=%async_computation.2 | async-start | bytes 1310720 | tf_op jit(solution)/shard_map/all_gather | solution.py:44
  8.0 373.9 %copy-start.3 = (bf16[5,2048,32]{1,2,0:T(8,128)(2,1)S(1)}, bf16[5,2048,32]{1,2,0:T(8,128)(2,1)}, u32[]{:S(2)}) copy-start(bf16[5,2048,32]{1,2,0:T(8,128)(2,1)} %param.15) | copy-start | bytes 1966084
  357.9 91.4 %reduce-scatter.3.cloned.1.call-start = ((), (), s32[]{:S(2)}) async-start(), calls=%async_computation.3 | async-start | bytes 2621440 | tf_op jit(solution)/shard_map/reduce_scatter | solution.py:54
  383.4 5.4 collective-permute-start
  388.9 6.6 collective-permute-start.1
  395.5 5.4 collective-permute-start.2
  400.9 5.3 collective-permute-start.3
  406.2 8.0 collective-permute-start.4
  414.1 2.0 copy-start.7
  414.1 2.0 copy-start.8
  414.2 2.1 copy-start.1
  416.1 1.0 copy-start.5
  416.1 748.4 %all-gather.5.cloned.1.call-start = ((), (), s32[]{:S(2)}) async-start(), calls=%async_computation.4 | async-start | bytes 1310720 | tf_op jit(solution)/shard_map/all_gather | solution.py:44
  420.8 28.4 %copy-start.6 = (f32[512]{0:T(512)S(1)}, f32[512]{0:T(512)}, u32[]{:S(2)}) copy-start(f32[512]{0:T(512)} %param.10) | copy-start | bytes 6148
  421.8 742.7 %copy-start.4 = (bf16[5,2048,32]{1,2,0:T(8,128)(2,1)S(1)}, bf16[5,2048,32]{1,2,0:T(8,128)(2,1)}, u32[]{:S(2)}) copy-start(bf16[5,2048,32]{1,2,0:T(8,128)(2,1)} %param.15) | copy-start | bytes 1966084
  1144.3 87.8 %reduce-scatter.5.cloned.1.call-start = ((), (), s32[]{:S(2)}) async-start(), calls=%async_computation.5 | async-start | bytes 2621440 | tf_op jit(solution)/shard_map/reduce_scatter | solution.py:54
  1166.0 5.4 collective-permute-start.5
  1171.5 6.6 collective-permute-start.6
  1178.1 5.4 collective-permute-start.7
  1183.5 5.3 collective-permute-start.8
  1188.8 8.1 collective-permute-start.9
  1196.9 1.9 copy-start.2
Sparse Core Ops, SparseCore 0:
  358.0 23.7 all-gather.2
  416.2 33.0 reduce-scatter.2
  1144.4 20.0 all-gather.4
  1199.0 33.0 reduce-scatter.4
